TPU v7x, 256 devices: a whole 4x4x8 slice. The times are simulated.
256 devices in a mesh: blk: 32 (over z, y_hi, core), grp: 8 (over y_lo, x).
Axes of the slice: x: 4, y: 4 (y_hi: 2, y_lo: 2; y = y_hi * 2 + y_lo), z: 8, core: 2. Of those that a mesh axis runs over, the one named last changes fastest.
Arguments:
- integrals: bfloat16 [128, 512, 1024], P('blk', None, 'grp'), may hold values from -1.1953125 to 1.1953125
- eps_occ: float32 [128], replicated, may hold values from -2 to -0.5
- eps_vir: float32 [512], replicated, may hold values from 0.3 to 3
- pair_mask: int32 [128, 4, 4], P('blk'), may hold values 0 or 1
Outputs:
- density: float32 [128, 512, 1024], P('blk', 'grp')
All inputs are finite; a program needn't handle non-finite values. No bound on the sum of `pair_mask` on one device may be relied on, other than what follows from the above.
Results may differ from a plain program's by a relative error of at most 0.0035.
Values may be sent and summed in bfloat16 or wider, within the bound.
A program may use at most 128 MiB of HBM per device.

v0:
```python
import jax
import jax.numpy as jnp
from jax import lax
from jax.sharding import Mesh
from jax.sharding import PartitionSpec as P

SHIFTS = 4
GRP = ("grp_0", "grp_1")


def shifted(block, axis, distance):
    devices = range(lax.axis_size(axis))
    route = [((i - distance) % len(devices), i) for i in devices]
    return lax.ppermute(block, axis, route)


def sum_in_order(parts, axes, turns):
    dims = [lax.axis_size(a) for a in axes]
    parts = parts.reshape(*dims, *parts.shape[1:])
    parts = parts.transpose(*turns, *range(len(axes), parts.ndim))
    parts = parts.reshape(-1, *parts.shape[len(axes) :])
    for k in turns:
        parts = lax.psum_scatter(parts, axes[k], scatter_dimension=0, tiled=True)
    return parts[0]


def split_up(value, dim, length):
    before, after = (value.shape[:dim], value.shape[dim + 1 :])
    return jnp.moveaxis(value.reshape(*before, length, -1, *after), dim, 0)


def summed_rows(value, axes, turns, dim):
    length = lax.axis_size(axes)
    return sum_in_order(split_up(value, dim, length), axes, turns)


def shards(integrals, eps_occ, eps_vir, pair_mask):
    occ_count = integrals.shape[0]
    groups = lax.axis_size(GRP)
    slab = eps_vir.shape[0] // groups
    rank = lax.axis_index(GRP)
    place = lax.axis_index("blk")
    cycle_size = lax.axis_size("blk")
    mine = lax.all_gather(integrals, GRP, axis=2, tiled=True)
    own_rows = lax.dynamic_slice_in_dim(mine, rank * slab, slab, 1)
    vir_rows = lax.dynamic_slice_in_dim(eps_vir, rank * slab, slab, 0)
    occ_mine = lax.dynamic_slice_in_dim(eps_occ, place * occ_count, occ_count, 0)
    density = jnp.zeros((occ_count, slab, mine.shape[2]), jnp.float32)
    carried = jnp.zeros((occ_count, slab, mine.shape[2]), jnp.float32)
    visiting = mine
    for step in range(1, SHIFTS + 1):
        visiting = shifted(visiting, "blk", 1)
        owner = (place - step) % cycle_size
        occ_visit = lax.dynamic_slice_in_dim(eps_occ, owner * occ_count, occ_count, 0)
        weights = pair_mask[:, step - 1, :].astype(jnp.float32)
        coulomb = jnp.einsum(
            "oap,lbp->olab", own_rows, visiting, preferred_element_type=jnp.float32
        )
        denom = (
            occ_mine[:, None, None, None]
            + occ_visit[None, :, None, None]
            - vir_rows[None, None, :, None]
            - eps_vir[None, None, None, :]
        )
        amplitude = (weights[:, :, None, None] * coulomb / denom).astype(jnp.bfloat16)
        density = density + jnp.einsum(
            "olab,lbp->oap", amplitude, visiting, preferred_element_type=jnp.float32
        )
        partial_terms = jnp.einsum(
            "olab,oap->lbp", amplitude, own_rows, preferred_element_type=jnp.float32
        )
        if step > 1:
            carried = shifted(carried, "blk", 1)
        contribution = summed_rows(partial_terms.astype(jnp.bfloat16), GRP, (1, 0), 1).astype(
            jnp.float32
        )
        carried = carried + contribution
    density = density + shifted(carried, "blk", -SHIFTS)
    return density


def solution(mesh):
    torus = Mesh(mesh.devices.reshape(mesh.shape["blk"], 2, 4), ("blk", "grp_0", "grp_1"))
    in_specs = (P("blk", None, GRP), P(), P(), P("blk", None, None))
    out_specs = P("blk", GRP, None)
    return jax.shard_map(
        shards, mesh=torus, in_specs=in_specs, out_specs=out_specs, check_vma=False
    )
```

profile of v0, /device:TPU:1, one launch (start us, length us, event | category | flops | bytes accessed | tf_op | source)
XLA Modules:
  0.0 508.0 jit_solution(16738053430705592444)
XLA Ops:
  7.3 66.5 %all-gather.2.cloned.1.call-done = bf16[4,512,1024]{2,1,0:T(8,128)(2,1)} async-done(((bf16[4,512,128]{2,1,0:T(8,128)(2,1)}), bf16[4,512,1024]{2,1,0:T(8,128)(2,1)}) %all-gather.2.cloned.1.call-update) | async-done | bytes 4194320 | tf_op jit(solution)/shard_map/all_gather | solution.py:44
  73.8 4.8 collective-permute-start
  81.2 43.1 %collective-permute-done = bf16[4,512,1024]{2,1,0:T(8,128)(2,1)} collective-permute-done((bf16[4,512,1024]{2,1,0:T(8,128)(2,1)}, bf16[4,512,1024]{2,1,0:T(8,128)(2,1)}, u32[]{:S(2)}, u32[]{:S(2)}) %collective-permute-start) | collective-permute-done | bytes 4194336 | tf_op jit(solution)/shard_map/ppermute | solution.py:14
  124.3 3.7 fusion.19
  133.2 4.1 collective-permute-start.1
  137.3 45.8 %collective-permute-done.1 = bf16[4,512,1024]{2,1,0:T(8,128)(2,1)S(1)} collective-permute-done((bf16[4,512,1024]{2,1,0:T(8,128)(2,1)}, bf16[4,512,1024]{2,1,0:T(8,128)(2,1)S(1)}, u32[]{:S(2)}, u32[]{:S(2)}) %collective-permute-start.1) | collective-permute-done | bytes 4194336 | tf_op jit(solution)/shard_map/ppermute | solution.py:14
  190.6 4.0 collective-permute-start.2
  194.6 45.8 %collective-permute-done.2 = bf16[4,512,1024]{2,1,0:T(8,128)(2,1)S(1)} collective-permute-done((bf16[4,512,1024]{2,1,0:T(8,128)(2,1)}, bf16[4,512,1024]{2,1,0:T(8,128)(2,1)S(1)}, u32[]{:S(2)}, u32[]{:S(2)}) %collective-permute-start.2) | collective-permute-done | bytes 4194336 | tf_op jit(solution)/shard_map/ppermute | solution.py:14
  248.0 4.1 collective-permute-start.3
  252.7 45.1 %collective-permute-done.3 = bf16[4,512,1024]{2,1,0:T(8,128)(2,1)} collective-permute-done((bf16[4,512,1024]{2,1,0:T(8,128)(2,1)}, bf16[4,512,1024]{2,1,0:T(8,128)(2,1)}, u32[]{:S(2)}, u32[]{:S(2)}) %collective-permute-start.3) | collective-permute-done | bytes 4194336 | tf_op jit(solution)/shard_map/ppermute | solution.py:14
  297.9 3.7 fusion.16
  307.5 23.6 %reduce-scatter.11.cloned.1.call-done = bf16[1,4,64,1024]{3,2,1,0:T(8,128)(2,1)} async-done(((bf16[2,4,64,1024]{3,2,1,0:T(8,128)(2,1)}), bf16[1,4,64,1024]{3,2,1,0:T(8,128)(2,1)}) %reduce-scatter.11.cloned.1.call-update) | async-done | bytes 524304 | tf_op jit(solution)/shard_map/reduce_scatter | solution.py:23
  335.3 14.2 %collective-permute-done.4 = f32[4,64,1024]{2,1,0:T(8,128)S(1)} collective-permute-done((f32[4,64,1024]{2,1,0:T(8,128)S(1)}, f32[4,64,1024]{2,1,0:T(8,128)S(1)}, u32[]{:S(2)}, u32[]{:S(2)}) %collective-permute-start.4) | collective-permute-done | bytes 1048608 | tf_op jit(solution)/shard_map/ppermute | solution.py:14
  349.5 10.3 %reduce-scatter.15.cloned.1.call-done = bf16[1,4,64,1024]{3,2,1,0:T(8,128)(2,1)} async-done(((bf16[2,4,64,1024]{3,2,1,0:T(8,128)(2,1)}), bf16[1,4,64,1024]{3,2,1,0:T(8,128)(2,1)}) %reduce-scatter.15.cloned.1.call-update) | async-done | bytes 524304 | tf_op jit(solution)/shard_map/reduce_scatter | solution.py:23
  362.0 3.8 collective-permute-start.5
  365.8 48.3 %reduce-scatter.21.cloned.1.call-done = bf16[2,4,64,1024]{3,2,1,0:T(8,128)(2,1)} async-done(((bf16[8,4,64,1024]{3,2,1,0:T(8,128)(2,1)}), bf16[2,4,64,1024]{3,2,1,0:T(8,128)(2,1)}) %reduce-scatter.21.cloned.1.call-update) | async-done | bytes 1048592 | tf_op jit(solution)/shard_map/reduce_scatter | solution.py:23
  414.1 27.6 %reduce-scatter.19.cloned.1.call-done = bf16[1,4,64,1024]{3,2,1,0:T(8,128)(2,1)} async-done(((bf16[2,4,64,1024]{3,2,1,0:T(8,128)(2,1)}), bf16[1,4,64,1024]{3,2,1,0:T(8,128)(2,1)}) %reduce-scatter.19.cloned.1.call-update) | async-done | bytes 524304 | tf_op jit(solution)/shard_map/reduce_scatter | solution.py:23
  442.9 3.1 collective-permute-start.6
  446.0 13.8 %collective-permute-done.6 = f32[4,64,1024]{2,1,0:T(8,128)S(1)} collective-permute-done((f32[4,64,1024]{2,1,0:T(8,128)S(1)}, f32[4,64,1024]{2,1,0:T(8,128)S(1)}, u32[]{:S(2)}, u32[]{:S(2)}) %collective-permute-start.6) | collective-permute-done | bytes 1048608 | tf_op jit(solution)/shard_map/ppermute | solution.py:14
  459.7 11.0 %reduce-scatter.23.cloned.1.call-done = bf16[1,4,64,1024]{3,2,1,0:T(8,128)(2,1)} async-done(((bf16[2,4,64,1024]{3,2,1,0:T(8,128)(2,1)}), bf16[1,4,64,1024]{3,2,1,0:T(8,128)(2,1)}) %reduce-scatter.23.cloned.1.call-update) | async-done | bytes 524304 | tf_op jit(solution)/shard_map/reduce_scatter | solution.py:23
  472.1 3.1 collective-permute-start.7
  475.2 3.8 fusion.28
  482.4 14.6 %collective-permute-done.7 = f32[4,64,1024]{2,1,0:T(8,128)S(1)} collective-permute-done((f32[4,64,1024]{2,1,0:T(8,128)S(1)}, f32[4,64,1024]{2,1,0:T(8,128)S(1)}, u32[]{:S(2)}, u32[]{:S(2)}) %collective-permute-start.7) | collective-permute-done | bytes 1048608 | tf_op jit(solution)/shard_map/ppermute | solution.py:14
  497.1 4.4 fusion.49
  (60 shorter events, 42.6 us)
Async XLA Ops:
  6.5 67.2 %all-gather.2.cloned.1.call-start = ((), (), s32[]{:S(2)}) async-start(), calls=%async_computation.8 | async-start | bytes 4718592 | tf_op jit(solution)/shard_map/all_gather | solution.py:44
  7.3 244.8 %reduce-scatter.9.cloned.1.call-start = ((), (), s32[]{:S(2)}) async-start(), calls=%async_computation.9 | async-start | bytes 5242880 | tf_op jit(solution)/shard_map/reduce_scatter | solution.py:23
  73.8 50.5 %collective-permute-start = (bf16[4,512,1024]{2,1,0:T(8,128)(2,1)}, bf16[4,512,1024]{2,1,0:T(8,128)(2,1)}, u32[]{:S(2)}, u32[]{:S(2)}) collective-permute-start(bf16[4,512,1024]{2,1,0:T(8,128)(2,1)} %all-gather.2.cloned.1.call-done), channel_id=1, source_target_pairs={{248,0},{0,8},{8,16},{16,24},{24,32},{32,40},{40,48},{48,56},{56,6... | collective-permute-start | bytes 12582920 | tf_op jit(solution)/shard_map/ppermute | solution.py:14
  128.0 2.7 copy-start.7
  133.1 49.9 %copy-start.6 = (f32[512]{0:T(512)S(1)}, f32[512]{0:T(512)}, u32[]{:S(2)}) copy-start(f32[512]{0:T(512)} %param.6) | copy-start | bytes 6148
  133.2 119.0 %reduce-scatter.13.cloned.1.call-start = ((), (), s32[]{:S(2)}) async-start(), calls=%async_computation.11 | async-start | bytes 5242880 | tf_op jit(solution)/shard_map/reduce_scatter | solution.py:23
  133.2 49.8 %collective-permute-start.1 = (bf16[4,512,1024]{2,1,0:T(8,128)(2,1)}, bf16[4,512,1024]{2,1,0:T(8,128)(2,1)S(1)}, u32[]{:S(2)}, u32[]{:S(2)}) collective-permute-start(bf16[4,512,1024]{2,1,0:T(8,128)(2,1)} %collective-permute-done), channel_id=1, source_target_pairs={{248,0},{0,8},{8,16},{16,24},{24,32},{32,40},{40,48},{48,56},{56,6... | collective-permute-start | bytes 12582920 | tf_op jit(solution)/shard_map/ppermute | solution.py:14
  183.0 2.7 copy-start
  190.5 116.2 %reduce-scatter.17.cloned.1.call-start = ((), (), s32[]{:S(2)}) async-start(), calls=%async_computation.13 | async-start | bytes 5242880 | tf_op jit(solution)/shard_map/reduce_scatter | solution.py:23
  190.6 49.8 %collective-permute-start.2 = (bf16[4,512,1024]{2,1,0:T(8,128)(2,1)}, bf16[4,512,1024]{2,1,0:T(8,128)(2,1)S(1)}, u32[]{:S(2)}, u32[]{:S(2)}) collective-permute-start(bf16[4,512,1024]{2,1,0:T(8,128)(2,1)} %copy-done), channel_id=1, source_target_pairs={{248,0},{0,8},{8,16},{16,24},{24,32},{32,40},{40,48},{48,56},{56,6... | collective-permute-start | bytes 12582920 | tf_op jit(solution)/shard_map/ppermute | solution.py:14
  240.3 2.8 copy-start.2
  247.9 83.1 %reduce-scatter.11.cloned.1.call-start = ((), (), s32[]{:S(2)}) async-start(), calls=%async_computation.10 | async-start | bytes 1572864 | tf_op jit(solution)/shard_map/reduce_scatter | solution.py:23
  248.0 49.9 %collective-permute-start.3 = (bf16[4,512,1024]{2,1,0:T(8,128)(2,1)}, bf16[4,512,1024]{2,1,0:T(8,128)(2,1)}, u32[]{:S(2)}, u32[]{:S(2)}) collective-permute-start(bf16[4,512,1024]{2,1,0:T(8,128)(2,1)} %copy-done.2), channel_id=1, source_target_pairs={{248,0},{0,8},{8,16},{16,24},{24,32},{32,40},{40,48},{48,56},{56,6... | collective-permute-start | bytes 12582920 | tf_op jit(solution)/shard_map/ppermute | solution.py:14
  252.1 107.7 %reduce-scatter.15.cloned.1.call-start = ((), (), s32[]{:S(2)}) async-start(), calls=%async_computation.12 | async-start | bytes 1572864 | tf_op jit(solution)/shard_map/reduce_scatter | solution.py:23
  252.7 161.4 %reduce-scatter.21.cloned.1.call-start = ((), (), s32[]{:S(2)}) async-start(), calls=%async_computation.15 | async-start | bytes 5242880 | tf_op jit(solution)/shard_map/reduce_scatter | solution.py:23
  301.5 2.7 copy-start.4
  306.7 135.0 %reduce-scatter.19.cloned.1.call-start = ((), (), s32[]{:S(2)}) async-start(), calls=%async_computation.14 | async-start | bytes 1572864 | tf_op jit(solution)/shard_map/reduce_scatter | solution.py:23
  307.4 163.3 %reduce-scatter.23.cloned.1.call-start = ((), (), s32[]{:S(2)}) async-start(), calls=%async_computation.16 | async-start | bytes 1572864 | tf_op jit(solution)/shard_map/reduce_scatter | solution.py:23
  332.2 17.3 %collective-permute-start.4 = (f32[4,64,1024]{2,1,0:T(8,128)S(1)}, f32[4,64,1024]{2,1,0:T(8,128)S(1)}, u32[]{:S(2)}, u32[]{:S(2)}) collective-permute-start(f32[4,64,1024]{2,1,0:T(8,128)S(1)} %bitcast_convert_fusion.4), channel_id=1, source_target_pairs={{248,0},{0,8},{8,16},{16,24},{24,32},{32,40},{40,48},{48,56},{56,6... | collective-permute-start | bytes 3145736 | tf_op jit(solution)/shard_map/ppermute | solution.py:14
  362.0 52.1 %collective-permute-start.5 = (f32[4,64,1024]{2,1,0:T(8,128)}, f32[4,64,1024]{2,1,0:T(8,128)S(1)}, u32[]{:S(2)}, u32[]{:S(2)}) collective-permute-start(f32[4,64,1024]{2,1,0:T(8,128)} %convert_add_fusion.2), channel_id=1, source_target_pairs={{248,0},{0,8},{8,16},{16,24},{24,32},{32,40},{40,48},{48,56},{56,6... | collective-permute-start | bytes 3145736 | tf_op jit(solution)/shard_map/ppermute | solution.py:14
  442.9 16.9 %collective-permute-start.6 = (f32[4,64,1024]{2,1,0:T(8,128)S(1)}, f32[4,64,1024]{2,1,0:T(8,128)S(1)}, u32[]{:S(2)}, u32[]{:S(2)}) collective-permute-start(f32[4,64,1024]{2,1,0:T(8,128)S(1)} %convert_add_fusion.1), channel_id=1, source_target_pairs={{248,0},{0,8},{8,16},{16,24},{24,32},{32,40},{40,48},{48,56},{56,6... | collective-permute-start | bytes 3145736 | tf_op jit(solution)/shard_map/ppermute | solution.py:14
  470.8 8.2 %copy-start.1 = (bf16[4,512,1024]{2,1,0:T(8,128)(2,1)S(1)}, bf16[4,512,1024]{2,1,0:T(8,128)(2,1)}, u32[]{:S(2)}) copy-start(bf16[4,512,1024]{2,1,0:T(8,128)(2,1)} %copy-done) | copy-start | bytes 12582916
  472.1 24.9 %collective-permute-start.7 = (f32[4,64,1024]{2,1,0:T(8,128)S(1)}, f32[4,64,1024]{2,1,0:T(8,128)S(1)}, u32[]{:S(2)}, u32[]{:S(2)}) collective-permute-start(f32[4,64,1024]{2,1,0:T(8,128)S(1)} %convert_add_fusion), channel_id=1, source_target_pairs={{32,0},{40,8},{48,16},{56,24},{64,32},{72,40},{80,48},{88,56},{96,... | collective-permute-start | bytes 3145736 | tf_op jit(solution)/shard_map/ppermute | solution.py:14
  481.2 15.9 %copy-start.5 = (bf16[4,4,64,512]{3,2,1,0:T(8,128)(2,1)S(1)}, bf16[4,4,64,512]{3,2,1,0:T(8,128)(2,1)}, u32[]{:S(2)}) copy-start(bf16[4,4,64,512]{3,2,1,0:T(8,128)(2,1)} %copy-done.4) | copy-start | bytes 3145732
  (1 other events, 2.2 us)
Sparse Core Ops, SparseCore 0:
  9.1 64.6 all-gather.1
  133.3 51.3 reduce-scatter.8
  190.6 53.2 reduce-scatter.12
  248.1 55.2 reduce-scatter.16
  305.9 25.1 reduce-scatter.10
  333.4 26.3 reduce-scatter.14
  362.5 51.4 reduce-scatter.20
  416.6 25.0 reduce-scatter.18
  444.3 26.4 reduce-scatter.22
where the time goes:
time: 509 us; the launch traced here: 508 us
  waiting for transfers between devices  412 us (81%)
  matrix products  33.6 us (7%)
  starting transfers between devices  30.4 us (6%)
  between operations  13.4 us (3%)
  local copies, waits for them, and re-layouts  12.2 us (2%)
  other arithmetic  6.84 us (1%)
    ppermute x8, waiting for transfers between devices, shifted(): return lax.ppermute(block, axis, route)  222 us
    reduce_scatter x8, waiting for transfers between devices, sum_in_order(): parts = lax.psum_scatter(parts, axes[k], scatter_dimension=0, tiled=True)  121 us
    all_gather x1, waiting for transfers between devices, shards(): mine = lax.all_gather(integrals, GRP, axis=2, tiled=True)  66.5 us
    ppermute x8, starting transfers between devices, shifted(): return lax.ppermute(block, axis, route)  30 us
    dot_general x4, matrix products, shards(): jnp.einsum('oap,lbp->olab', own_rows, visiting, preferred_element_type=jn...  12.8 us
    dot_general x4, matrix products, shards(): jnp.einsum('olab,lbp->oap', amplitude, visiting, preferred_element_type=j...  10.7 us
  transfers between devices with their start and end apart: 17, of which 13 were waited for; matrix products, arithmetic and copies ran while one was open for 7% of the time, Pallas kernels for 0%

commit v1 on v0

v1 whole, which is shorter than its diff:
```python
import jax
import jax.numpy as jnp
from jax import lax
from jax.experimental import pallas as pl
from jax.experimental.pallas import tpu as pltpu
from jax.sharding import PartitionSpec as P

MESH = pl.DeviceIdType.MESH
F32 = jnp.float32
BF16 = jnp.bfloat16
OCC = 4
NVIR = 512
NAUX = 1024
HALF = 256
QUART = 128
SLAB = 64
SIDE = 512
KEYS = OCC * QUART
CHUNK = 256
N_SEM = 80


def kernel(
    b_ref, eo_ref, ev_ref, mask_ref, out_ref,
    kb, qb, acc, rowb, nevb, wbuf, wsend, osend, orecv, ssem, rsem, lsem,
):
    k = lax.axis_index("blk")
    g = lax.axis_index("grp")
    nblk = lax.axis_size("blk")
    u = k % 4
    z = k // 4
    nz = nblk // 4
    yh, c = u // 2, u % 2
    yl, x = g // 4, g % 4
    y = 2 * yh + yl

    def at_y(step):
        t = (y + step) % 4
        return t, (4 * z + 2 * (t // 2) + c, 4 * (t % 2) + x)

    def at_z(step):
        return (4 * ((z + nz + step) % nz) + u, g)

    def at_x(step):
        t = (x + step) % 4
        return t, (k, 4 * yl + t)

    def at_blk(step):
        return ((k + nblk + step) % nblk, g)

    mate = (4 * z + 2 * yh + (1 - c), g)
    other_half = (k, 4 * (1 - yl) + x)
    _, up_y = at_y(1)
    _, down_y = at_y(3)

    barrier = pltpu.get_barrier_semaphore()
    peers = [at_x(1)[1], at_x(2)[1], at_x(3)[1], up_y, down_y]
    peers += [at_blk(s) for s in (1, 2, 3, 4, -1, -2, -3, -4)]
    for dev in peers:
        pl.semaphore_signal(barrier, inc=1, device_id=dev, device_id_type=MESH)
    pl.semaphore_wait(barrier, len(peers))

    sent = []

    def descriptor(i, src, dst, dev):
        return pltpu.make_async_remote_copy(
            src_ref=src, dst_ref=dst, send_sem=ssem.at[i], recv_sem=rsem.at[i],
            device_id=dev, device_id_type=MESH,
        )

    def send(i, src, dst, dev):
        copy = descriptor(i, src, dst, dev)
        copy.start()
        sent.append(copy)

    def arrived(i, ref):
        descriptor(i, ref, ref, mate).wait_recv()

    counter = iter(range(N_SEM))

    def new(n):
        return [next(counter) for _ in range(n)]

    cols = pl.ds(pl.multiple_of(g * 128, 128), 128)
    q_rows = lambda half: pl.ds(pl.multiple_of(half * HALF, HALF), HALF)
    k_rows = lambda quart: pl.ds(pl.multiple_of(quart * QUART, QUART), QUART)

    def unit(plane, t, o0, no):
        slot = 4 * (plane + 1) + 2 * (t // 2) + c
        return kb.at[slot, pl.ds(o0, no), :, pl.ds(pl.multiple_of((t % 2) * SIDE, SIDE), SIDE)]

    s1 = new(3)
    for t in (1, 2, 3):
        xt, dev = at_x(t)
        send(s1[t - 1], b_ref.at[:, k_rows(xt), :], kb.at[4 + u, :, :, cols], dev)
    l1 = pltpu.make_async_copy(b_ref.at[:, k_rows(x), :], kb.at[4 + u, :, :, cols], lsem.at[0])
    l1.start()
    (q1,) = new(1)
    send(q1, b_ref.at[:, q_rows(1 - yl), :], qb.at[:, :, cols], other_half)
    q2 = new(3)
    for t in (1, 2, 3):
        send(q2[t - 1], b_ref.at[:, q_rows(yl), :], qb.at[:, :, cols], at_x(t)[1])
    l2 = pltpu.make_async_copy(b_ref.at[:, q_rows(yl), :], qb.at[:, :, cols], lsem.at[1])
    l2.start()

    for s in range(1, 5):
        for o in range(OCC):
            for l in range(OCC):
                lanes = pl.ds(l * QUART, QUART)
                wbuf[4 - s, pl.ds(o, 1), lanes] = jnp.full((1, QUART), mask_ref[o, s - 1, l].astype(F32), F32)
                wsend[s - 1, pl.ds(o, 1), lanes] = jnp.full((1, QUART), mask_ref[l, s - 1, o].astype(F32), F32)
    wsem = new(4)
    for s in range(1, 5):
        send(wsem[s - 1], wsend.at[s - 1], wbuf.at[4 + s], at_blk(-s))
    evq = ev_ref[pl.ds(x, 1), :]
    for d in range(9):
        j = (k + nblk + d - 4) % nblk
        for o in range(OCC):
            for l in range(OCC):
                e = eo_ref[OCC * k + o] + eo_ref[OCC * j + l]
                rowb[d, pl.ds(o, 1), pl.ds(l * QUART, QUART)] = e - evq
    for h in range(2):
        row = ev_ref[pl.ds(2 * yl + h, 1), :]
        nevb[pl.ds(h * 128, 128), :] = jnp.transpose(jnp.broadcast_to(row, (128, 128)))
    acc[...] = jnp.zeros_like(acc)

    l1.wait()
    for t in (1, 2, 3):
        xt, _ = at_x(4 - t)
        arrived(s1[t - 1], kb.at[4 + u, :, :, pl.ds(pl.multiple_of((4 * yl + xt) * 128, 128), 128)])

    a1 = new(2)
    b1y = new(2)
    b1z = new(2)
    a3o = new(2)
    a3 = new(6)
    a2 = new(2)
    b2 = new(4)
    b3 = new(6)
    dd = new(24)
    dd_i = iter(dd)
    mates = []

    def to_mate(plane, step, o0, no):
        t, _ = at_y(step)
        i = next(dd_i)
        ref = unit(plane, t, o0, no)
        send(i, ref, ref, mate)
        slot = 4 * (plane + 1) + 2 * (t // 2) + (1 - c)
        half = pl.ds(pl.multiple_of((t % 2) * SIDE, SIDE), SIDE)
        mates.append((i, kb.at[slot, pl.ds(o0, no), :, half]))

    def y_copy(i, plane, origin, o0, no, dev):
        ref = unit(plane, origin, o0, no)
        send(i, ref, ref, dev)

    def z_copy(i, origin, o0, no, step):
        send(i, unit(0, origin, o0, no), unit(-step, origin, o0, no), at_z(step))

    y_up, _ = at_y(1)
    y_dn, _ = at_y(3)
    y_far, _ = at_y(2)
    for i, dev in zip(a1, (up_y, down_y)):
        y_copy(i, 0, y, 0, 2, dev)
    for i, step in zip(b1z, (1, -1)):
        z_copy(i, y, 2, 2, step)
    for i, step in zip(a3o, (1, -1)):
        z_copy(i, y, 0, 2, step)
    for i, dev in zip(b1y, (up_y, down_y)):
        y_copy(i, 0, y, 2, 2, dev)
    to_mate(0, 0, 0, 2)
    to_mate(0, 0, 2, 2)

    other_cols = pl.ds(pl.multiple_of((4 * (1 - yl) + x) * 128, 128), 128)
    arrived(q1, qb.at[:, :, other_cols])
    q3 = new(3)
    for t in (1, 2, 3):
        ref = qb.at[:, :, other_cols]
        send(q3[t - 1], ref, ref, at_x(t)[1])

    arrived(a1[0], unit(0, y_dn, 0, 2))
    y_copy(a2[0], 0, y_dn, 0, 1, up_y)
    z_copy(a3[0], y_dn, 0, 2, 1)
    z_copy(a3[1], y_dn, 0, 2, -1)
    to_mate(0, 3, 0, 2)
    arrived(a1[1], unit(0, y_up, 0, 2))
    y_copy(a2[1], 0, y_up, 1, 1, down_y)
    z_copy(a3[2], y_up, 0, 2, 1)
    z_copy(a3[3], y_up, 0, 2, -1)
    to_mate(0, 1, 0, 2)
    for n, plane in enumerate((-1, 1)):
        arrived(b1z[n], unit(plane, y, 2, 2))
        y_copy(b2[2 * n], plane, y, 2, 2, up_y)
        y_copy(b2[2 * n + 1], plane, y, 2, 2, down_y)
        to_mate(plane, 0, 2, 2)
    arrived(b1y[0], unit(0, y_dn, 2, 2))
    y_copy(b3[0], 0, y_dn, 2, 1, up_y)
    to_mate(0, 3, 2, 2)
    arrived(b1y[1], unit(0, y_up, 2, 2))
    y_copy(b3[1], 0, y_up, 3, 1, down_y)
    to_mate(0, 1, 2, 2)

    l2.wait()
    for t in (1, 2, 3):
        xt, _ = at_x(4 - t)
        arrived(q2[t - 1], qb.at[:, :, pl.ds(pl.multiple_of((4 * yl + xt) * 128, 128), 128)])
        arrived(q3[t - 1], qb.at[:, :, pl.ds(pl.multiple_of((4 * (1 - yl) + xt) * 128, 128), 128)])

    arrived(a2[0], unit(0, y_far, 0, 1))
    arrived(a2[1], unit(0, y_far, 1, 1))
    z_copy(a3[4], y_far, 0, 2, 1)
    z_copy(a3[5], y_far, 0, 2, -1)
    to_mate(0, 2, 0, 2)
    for n, plane in enumerate((-1, 1)):
        arrived(b2[2 * n], unit(plane, y_dn, 2, 2))
        y_copy(b3[2 + 2 * n], plane, y_dn, 2, 1, up_y)
        to_mate(plane, 3, 2, 2)
        arrived(b2[2 * n + 1], unit(plane, y_up, 2, 2))
        y_copy(b3[3 + 2 * n], plane, y_up, 3, 1, down_y)
        to_mate(plane, 1, 2, 2)
    arrived(b3[0], unit(0, y_far, 2, 1))
    arrived(b3[1], unit(0, y_far, 3, 1))
    to_mate(0, 2, 2, 2)

    def arrive_mates(n):
        for i, ref in mates[:n]:
            arrived(i, ref)
        del mates[:n]

    for s in range(1, 5):
        arrived(wsem[s - 1], wbuf.at[4 + s])

    def block(slot, a0):
        d = slot - u
        keys = kb[slot].reshape(KEYS, NAUX)
        q = qb[:, pl.ds(a0, CHUNK), :].reshape(OCC * CHUNK, NAUX)
        s = lax.dot_general(q, keys, (((1,), (1,)), ((), ())), preferred_element_type=F32)
        nev = nevb[pl.ds(a0, CHUNK), :]
        nev = jnp.concatenate([nev] * OCC, axis=1)
        parts = []
        for o in range(OCC):
            den = rowb[d, pl.ds(o, 1), :] - nev
            w = wbuf[d, pl.ds(o, 1), :]
            parts.append((s[o * CHUNK : (o + 1) * CHUNK] * w / den).astype(BF16))
        amp = jnp.concatenate(parts, axis=0)
        acc[:, pl.ds(a0, CHUNK), :] += jnp.dot(amp, keys, preferred_element_type=F32).reshape(OCC, CHUNK, NAUX)

    def blocks(slot_of, n):
        def body(i, _):
            block(slot_of(i // (HALF // CHUNK)), pl.multiple_of((i % (HALF // CHUNK)) * CHUNK, CHUNK))
            return 0
        lax.fori_loop(0, n * (HALF // CHUNK), body, 0)

    arrive_mates(len(mates))
    blocks(lambda i: 4 + (u + 1 + i) % 4, 3)

    for n, step in enumerate((1, -1)):
        plane = -step
        arrived(a3o[n], unit(plane, y, 0, 2))
        to_mate(plane, 0, 0, 2)
        arrived(a3[n], unit(plane, y_dn, 0, 2))
        to_mate(plane, 3, 0, 2)
        arrived(a3[2 + n], unit(plane, y_up, 0, 2))
        to_mate(plane, 1, 0, 2)
        arrived(a3[4 + n], unit(plane, y_far, 0, 2))
        to_mate(plane, 2, 0, 2)
        arrived(b3[2 + 2 * n], unit(plane, y_far, 2, 1))
        arrived(b3[3 + 2 * n], unit(plane, y_far, 3, 1))
        to_mate(plane, 2, 2, 2)
    arrive_mates(len(mates))

    def outer(i):
        p = (u + i) % 4
        near = jnp.where(p >= u, p, 8 + p)
        return jnp.where(i == 4, 8 + u, near)

    blocks(outer, 5)

    osem = new(3)
    for t in (2, 1, 3):
        xt, dev = at_x(t)
        rows = pl.ds(pl.multiple_of(xt * SLAB, SLAB), SLAB)
        osend[t - 1] = acc[:, rows, :].astype(BF16)
        send(osem[t - 1], osend.at[t - 1], orecv.at[t - 1], dev)
    rows = pl.ds(pl.multiple_of(x * SLAB, SLAB), SLAB)
    total = acc[:, rows, :]
    for t in (1, 3, 2):
        arrived(osem[t - 1], orecv.at[t - 1])
        total = total + orecv[t - 1].astype(F32)
    out_ref[...] = total
    for copy in sent:
        copy.wait_send()


def shards(integrals, eps_occ, eps_vir, pair_mask):
    vmem = pl.BlockSpec(memory_space=pltpu.VMEM)
    smem = pl.BlockSpec(memory_space=pltpu.SMEM)
    return pl.pallas_call(
        kernel,
        out_shape=jax.ShapeDtypeStruct((OCC, SLAB, NAUX), F32),
        in_specs=[pl.BlockSpec(memory_space=pl.ANY), smem, vmem, smem],
        out_specs=vmem,
        scratch_shapes=[
            pltpu.VMEM((12, OCC, QUART, NAUX), BF16),
            pltpu.VMEM((OCC, HALF, NAUX), BF16),
            pltpu.VMEM((OCC, HALF, NAUX), F32),
            pltpu.VMEM((9, 8, KEYS), F32),
            pltpu.VMEM((HALF, 128), F32),
            pltpu.VMEM((9, 8, KEYS), F32),
            pltpu.VMEM((4, 8, KEYS), F32),
            pltpu.VMEM((3, OCC, SLAB, NAUX), BF16),
            pltpu.VMEM((3, OCC, SLAB, NAUX), BF16),
            pltpu.SemaphoreType.DMA((N_SEM,)),
            pltpu.SemaphoreType.DMA((N_SEM,)),
            pltpu.SemaphoreType.DMA((2,)),
        ],
        compiler_params=pltpu.CompilerParams(
            collective_id=0, has_side_effects=True, vmem_limit_bytes=56 * 1024 * 1024
        ),
        name="amplitudes",
    )(integrals, eps_occ, eps_vir.reshape(4, 128), pair_mask)


def solution(mesh):
    return jax.shard_map(
        shards,
        mesh=mesh,
        in_specs=(P("blk", None, "grp"), P(), P(), P("blk", None, None)),
        out_specs=P("blk", "grp", None),
        check_vma=False,
    )
```

time: 509 us -> 104 us (0.20)
  waiting for transfers between devices: 412 us -> 0 us
  Pallas kernels: 0 us -> 101 us
  matrix products: 33.6 us -> 0 us
  starting transfers between devices: 30.4 us -> 0 us
  between operations: 13.4 us -> 0.01 us
  local copies, waits for them, and re-layouts: 12.2 us -> 2.31 us
  other arithmetic: 6.84 us -> 0 us
    ppermute x8 -> x0, waiting for transfers between devices: 222 us -> none  [shifted(): return lax.ppermute(block, axis, route)]
    reduce_scatter x8 -> x0, waiting for transfers between devices: 121 us -> none  [sum_in_order(): parts = lax.psum_scatter(parts, axes[k], scatter_dimension=0, tiled=True)]
    pallas_call x0 -> x1, Pallas kernels: none -> 101 us  [shards(): pl.pallas_call(kernel, out_shape=jax.ShapeDtypeStruct((OCC, SLAB, NAUX),...]
    all_gather x1 -> x0, waiting for transfers between devices: 66.5 us -> none  [shards(): mine = lax.all_gather(integrals, GRP, axis=2, tiled=True)]
    dot_general x12 -> x0, matrix products: 33.6 us -> none  [the longest x4 12.8 us: shards(): jnp.einsum('oap,lbp->olab', own_rows, visiting, preferred_element_type=jn...]
    ppermute x8 -> x0, starting transfers between devices: 30 us -> none  [shifted(): return lax.ppermute(block, axis, route)]
    transpose x4 -> x0, local copies, waits for them, and re-layouts: 9.62 us -> none  [sum_in_order(): parts = parts.transpose(*turns, *range(len(axes), parts.ndim))]
  transfers between devices with their start and end apart: 17 -> 0, of which waited for: 13 -> 0; matrix products, arithmetic and copies ran while one was open for 7% -> 0% of each run, Pallas kernels for 0% -> 0%
where the time goes in v1:
time: 104 us; the launch traced here: 103 us
  Pallas kernels  101 us (97%)
  local copies, waits for them, and re-layouts  2.31 us (2%)
    pallas_call x1, Pallas kernels, shards(): pl.pallas_call(kernel, out_shape=jax.ShapeDtypeStruct((OCC, SLAB, NAUX),...  101 us
    unnamed x1, local copies, waits for them, and re-layouts  2.31 us

profile of v1, /device:TPU:1, one launch (start us, length us, event | category | flops | bytes accessed | tf_op | source)
XLA Modules:
  0.0 103.2 jit_solution(5341302306266547807)
XLA Ops:
  0.0 100.9 %amplitudes.1 = f32[4,64,1024]{2,1,0:T(8,128)} custom-call(bf16[4,512,128]{2,1,0:T(8,128)(2,1)} %b_ref.1, f32[128]{0:T(128)} %eo_ref.1, f32[4,128]{1,0:T(4,128)} %bitcast.1, s32[4,4,4]{2,1,0:T(4,128)} %mask_ref.1), custom_call_target="tpu_custom_call" | custom-call | tf_op jit(solution)/shard_map/amplitudes/pallas_call | solution.py:298
  100.9 2.3 %copy.6 = f32[4,64,1024]{2,1,0:T(8,128)} copy(f32[4,64,1024]{2,1,0:T(8,128)} %amplitudes.1) | data formatting | bytes 2097152

commit v2 on v0

v2 whole, which is shorter than its diff:
```python
import jax
import jax.numpy as jnp
from jax import lax
from jax.experimental import pallas as pl
from jax.experimental.pallas import tpu as pltpu
from jax.sharding import PartitionSpec as P

MESH = pl.DeviceIdType.MESH
F32 = jnp.float32
BF16 = jnp.bfloat16
OCC = 4
NVIR = 512
NAUX = 1024
HALF = 256
QUART = 128
SLAB = 64
SIDE = 512
KEYS = OCC * QUART
N_SEM = 72


def kernel(
    b_ref, eo_ref, ev_ref, mask_ref, out_ref,
    kb, qb, acc, rowb, nevb, wbuf, wsend, osend, orecv, ssem, rsem, lsem,
):
    k = lax.axis_index("blk")
    g = lax.axis_index("grp")
    nblk = lax.axis_size("blk")
    u = k % 4
    z = k // 4
    nz = nblk // 4
    yh, c = u // 2, u % 2
    yl, x = g // 4, g % 4

    def at_z(step):
        return (4 * ((z + nz + step) % nz) + u, g)

    def at_x(step):
        return (k, 4 * yl + (x + step) % 4)

    def at_blk(step):
        return ((k + nblk + step) % nblk, g)

    mate = (k + 1 - 2 * c, g)
    lo = (k, 4 * (1 - yl) + x)
    hi = (4 * z + (u + 2) % 4, 4 * (1 - yl) + x)
    right, left = at_x(1), at_x(3)

    barrier = pltpu.get_barrier_semaphore()
    peers = [at_x(1), at_x(2), at_x(3), lo, hi]
    peers += [at_blk(s) for s in (1, 2, 3, 4, -1, -2, -3, -4)]
    for dev in peers:
        pl.semaphore_signal(barrier, inc=1, device_id=dev, device_id_type=MESH)
    pl.semaphore_wait(barrier, len(peers))

    sent = []
    sems = {}

    def descriptor(name, src, dst, dev):
        i = sems.setdefault(name, len(sems))
        return pltpu.make_async_remote_copy(
            src_ref=src, dst_ref=dst, send_sem=ssem.at[i], recv_sem=rsem.at[i],
            device_id=dev, device_id_type=MESH,
        )

    def send(name, src, dst, dev):
        copy = descriptor(name, src, dst, dev)
        copy.start()
        sent.append(copy)

    def arrived(name, ref):
        descriptor(name, ref, ref, mate).wait_recv()

    def part(start, size):
        return pl.ds(pl.multiple_of(start, size), size)

    own, mown = 4 + u, 5 + u - 2 * c
    mu = mown - 4
    s2, s4 = 2 - 4 * yh, 4 - 8 * yh
    below, above = u, 8 + u
    cross, mcross = own + s2, mown + s2
    diag, mdiag = own - s2, mown - s2
    dsend = own + s4
    zshare, mzshare = u + 8 * (1 - c), mu + 8 * c

    def unit(slot, half, pr):
        return kb.at[slot, pl.ds(2 * pr, 2), :, part(half * SIDE, SIDE)]

    def whole(slot, pr):
        return kb.at[slot, pl.ds(2 * pr, 2)]

    def slice_of(t):
        return part(((4 * yl) + (x + t) % 4) * 128, 128)

    def other_slice_of(t):
        return part((4 * (1 - yl) + (x + t) % 4) * 128, 128)

    cols = slice_of(0)

    def q_part(h):
        return pl.ds(h * 128, 128)

    local = []
    for pr in range(2):
        for t in (1, 3, 2):
            rows = part((x + t) % 4 * QUART, QUART)
            send(("s1", pr, t), b_ref.at[pl.ds(2 * pr, 2), rows, :], kb.at[own, pl.ds(2 * pr, 2), :, cols], at_x(t))
        rows = part(x * QUART, QUART)
        copy = pltpu.make_async_copy(b_ref.at[pl.ds(2 * pr, 2), rows, :], kb.at[own, pl.ds(2 * pr, 2), :, cols], lsem.at[pr])
        copy.start()
        local.append(copy)
    for h in range(2):
        send(("q1", h), b_ref.at[:, part((1 - yl) * HALF + h * 128, 128), :], qb.at[:, q_part(h), cols], lo)

    def queries(h):
        for t in (1, 3, 2):
            send(("q2", h, t), b_ref.at[:, part(yl * HALF + h * 128, 128), :], qb.at[:, q_part(h), cols], at_x(t))

    def queries_other(h):
        ref = qb.at[:, q_part(h), other_slice_of(0)]
        arrived(("q1", h), ref)
        for t in (1, 3, 2):
            send(("q3", h, t), ref, ref, at_x(t))

    def queries_arrived(h):
        local[2 + h].wait()
        for t in (1, 3, 2):
            arrived(("q2", h, t), qb.at[:, q_part(h), slice_of(4 - t)])
            arrived(("q3", h, t), qb.at[:, q_part(h), other_slice_of(4 - t)])

    queries(0)
    for h in range(2):
        copy = pltpu.make_async_copy(b_ref.at[:, part(yl * HALF + h * 128, 128), :], qb.at[:, q_part(h), cols], lsem.at[2 + h])
        copy.start()
        local.append(copy)

    for s in range(1, 5):
        for o in range(OCC):
            for l in range(OCC):
                lanes = pl.ds(l * QUART, QUART)
                wbuf[4 - s, pl.ds(o, 1), lanes] = jnp.full((1, QUART), mask_ref[o, s - 1, l].astype(F32), F32)
                wsend[s - 1, pl.ds(o, 1), lanes] = jnp.full((1, QUART), mask_ref[l, s - 1, o].astype(F32), F32)
    for s in range(1, 5):
        send(("w", s), wsend.at[s - 1], wbuf.at[4 + s], at_blk(-s))
    evq = ev_ref[pl.ds(x, 1), :]
    for d in range(9):
        j = (k + nblk + d - 4) % nblk
        for o in range(OCC):
            for l in range(OCC):
                e = eo_ref[OCC * k + o] + eo_ref[OCC * j + l]
                rowb[d, pl.ds(o, 1), pl.ds(l * QUART, QUART)] = e - evq
    for h in range(2):
        row = ev_ref[pl.ds(2 * yl + h, 1), :]
        nevb[pl.ds(h * 128, 128), :] = jnp.transpose(jnp.broadcast_to(row, (128, 128)))
    acc[...] = jnp.zeros_like(acc)

    def own_ready(pr):
        local[pr].wait()
        for t in (1, 3, 2):
            arrived(("s1", pr, t), kb.at[own, pl.ds(2 * pr, 2), :, slice_of(4 - t)])
        ref = unit(own, yl, pr)
        send(("hi", pr), ref, ref, hi)
        send(("lo", pr), ref, ref, lo)
        for step in (1, -1):
            send(("z", step, pr), ref, unit(own - 4 * step, yl, pr), at_z(step))

    def to_mate(name, slot, pr):
        send((name, pr), whole(slot, pr), whole(slot, pr), mate)

    def lo_ready(pr):
        ref = unit(own, 1 - yl, pr)
        arrived(("lo", pr), ref)
        for step in (1, -1):
            send(("zz", step, pr), ref, unit(own - 4 * step, 1 - yl, pr), at_z(step))
        to_mate("mown", own, pr)

    def hi_ready(pr):
        ref = unit(cross, 1 - yl, pr)
        arrived(("hi", pr), ref)
        send(("loc", pr), ref, ref, lo)

    def z_ready(pr):
        for step in (1, -1):
            arrived(("z", step, pr), unit(own - 4 * step, yl, pr))
        ref = unit(dsend, yl, pr)
        send(("hid", pr), ref, ref, hi)

    def zz_ready(pr):
        for step in (1, -1):
            arrived(("zz", step, pr), unit(own - 4 * step, 1 - yl, pr))
        if pr == 1:
            ref = unit(dsend, 1 - yl, pr)
            send(("hie", pr), ref, ref, hi)
        to_mate("mz", zshare, pr)

    def cross_ready(pr):
        arrived(("loc", pr), unit(cross, yl, pr))
        to_mate("mcross", cross, pr)

    def hid_ready():
        ref = unit(diag, 1 - yl, 0)
        arrived(("hid", 0), ref)
        send(("lod", 0), ref, ref, lo)

    def diag_ready(pr):
        if pr == 0:
            arrived(("lod", 0), unit(diag, yl, 0))
        else:
            arrived(("hid", 1), unit(diag, 1 - yl, 1))
            arrived(("hie", 1), unit(diag, yl, 1))
        to_mate("mdiag", diag, pr)

    def from_mate(name, slot, pr):
        arrived((name, pr), whole(slot, pr))

    def pick(i, values):
        value = values[-1]
        for n in range(len(values) - 2, -1, -1):
            value = jnp.where(i == n, values[n], value)
        return value

    def compute(units, a0, na):
        def body(i, _):
            rows = pl.ds(a0, na)
            q = qb[:, rows, :].reshape(OCC * na, NAUX)
            nev = nevb[rows, :]
            nev = jnp.concatenate([nev] * 2, axis=1)
            total = None
            for n in range(2):
                slot = pick(i, [unit[n][0] for unit in units])
                pr = pick(i, [unit[n][1] for unit in units])
                d = slot - u
                keys = kb[slot, pl.ds(2 * pr, 2)].reshape(2 * QUART, NAUX)
                s = lax.dot_general(q, keys, (((1,), (1,)), ((), ())), preferred_element_type=F32)
                lanes = part(pr * 256, 256)
                amps = []
                for o in range(OCC):
                    den = rowb[d, pl.ds(o, 1), lanes] - nev
                    w = wbuf[d, pl.ds(o, 1), lanes]
                    amps.append((s[o * na : (o + 1) * na] * w / den).astype(BF16))
                amp = jnp.concatenate(amps, axis=0)
                term = jnp.dot(amp, keys, preferred_element_type=F32)
                total = term if total is None else total + term
            acc[:, rows, :] += total.reshape(OCC, na, NAUX)
            return 0

        lax.fori_loop(0, len(units), body, 0)

    u0 = ((mown, 0), (mown, 1))
    u1 = ((cross, 0), (below, 0))
    u2 = ((above, 0), (mzshare, 0))
    u3 = ((mcross, 0), (cross, 1))
    u4 = ((below, 1), (above, 1))
    u5 = ((mzshare, 1), (mcross, 1))
    u6 = ((diag, 0), (diag, 1))
    u7 = ((mdiag, 0), (mdiag, 1))

    own_ready(0)
    queries_other(0)
    own_ready(1)
    queries(1)
    queries_other(1)
    lo_ready(0)
    hi_ready(0)
    z_ready(0)
    lo_ready(1)
    hi_ready(1)
    z_ready(1)
    for s in range(1, 5):
        arrived(("w", s), wbuf.at[4 + s])
    from_mate("mown", mown, 0)
    from_mate("mown", mown, 1)
    queries_arrived(0)
    compute([u0], 0, 128)
    zz_ready(0)
    cross_ready(0)
    hid_ready()
    compute([u1], 0, 128)
    from_mate("mz", mzshare, 0)
    from_mate("mcross", mcross, 0)
    compute([u2], 0, 128)
    zz_ready(1)
    cross_ready(1)
    queries_arrived(1)
    compute([u0, u1, u2], 128, 128)
    diag_ready(0)
    from_mate("mz", mzshare, 1)
    from_mate("mcross", mcross, 1)
    compute([u3, u4], 0, 256)
    diag_ready(1)
    compute([u5], 0, 256)
    for pr in range(2):
        from_mate("mdiag", mdiag, pr)
    late = [u6, u7]

    def slab(t):
        return part((x + t) % 4 * SLAB, SLAB)

    def finish(t):
        compute(late, pl.multiple_of((x + t) % 4 * SLAB, SLAB), SLAB)

    def push(n, value, dev):
        osend[n] = value.astype(BF16)
        send(("o", n), osend.at[n], orecv.at[n], dev)

    first_two, last_two = slice(0, 2), slice(2, 4)
    finish(2)
    push(0, acc[first_two, slab(2), :], right)
    push(1, acc[last_two, slab(2), :], left)
    finish(1)
    push(2, acc[last_two, slab(1), :], right)
    finish(3)
    push(3, acc[first_two, slab(3), :], left)
    arrived(("o", 0), orecv.at[0])
    push(4, acc[first_two, slab(1), :] + orecv[0].astype(F32), right)
    arrived(("o", 1), orecv.at[1])
    push(5, acc[last_two, slab(3), :] + orecv[1].astype(F32), left)
    finish(0)
    for n in (2, 3):
        arrived(("o", n), orecv.at[n])
    arrived(("o", 4), orecv.at[4])
    out_ref[first_two] = acc[first_two, slab(0), :] + orecv[3].astype(F32) + orecv[4].astype(F32)
    arrived(("o", 5), orecv.at[5])
    out_ref[last_two] = acc[last_two, slab(0), :] + orecv[2].astype(F32) + orecv[5].astype(F32)
    for copy in sent:
        copy.wait_send()


def shards(integrals, eps_occ, eps_vir, pair_mask):
    vmem = pl.BlockSpec(memory_space=pltpu.VMEM)
    smem = pl.BlockSpec(memory_space=pltpu.SMEM)
    return pl.pallas_call(
        kernel,
        out_shape=jax.ShapeDtypeStruct((OCC, SLAB, NAUX), F32),
        in_specs=[pl.BlockSpec(memory_space=pl.ANY), smem, vmem, smem],
        out_specs=vmem,
        scratch_shapes=[
            pltpu.VMEM((12, OCC, QUART, NAUX), BF16),
            pltpu.VMEM((OCC, HALF, NAUX), BF16),
            pltpu.VMEM((OCC, HALF, NAUX), F32),
            pltpu.VMEM((9, 8, KEYS), F32),
            pltpu.VMEM((HALF, 128), F32),
            pltpu.VMEM((9, 8, KEYS), F32),
            pltpu.VMEM((4, 8, KEYS), F32),
            pltpu.VMEM((6, 2, SLAB, NAUX), BF16),
            pltpu.VMEM((6, 2, SLAB, NAUX), BF16),
            pltpu.SemaphoreType.DMA((N_SEM,)),
            pltpu.SemaphoreType.DMA((N_SEM,)),
            pltpu.SemaphoreType.DMA((4,)),
        ],
        compiler_params=pltpu.CompilerParams(
            collective_id=0, has_side_effects=True, vmem_limit_bytes=56 * 1024 * 1024
        ),
        name="amplitudes",
    )(integrals, eps_occ, eps_vir.reshape(4, 128), pair_mask)


def solution(mesh):
    return jax.shard_map(
        shards,
        mesh=mesh,
        in_specs=(P("blk", None, "grp"), P(), P(), P("blk", None, None)),
        out_specs=P("blk", "grp", None),
        check_vma=False,
    )
```

time: 509 us -> 78.9 us (0.16)
  waiting for transfers between devices: 412 us -> 0 us
  Pallas kernels: 0 us -> 76.4 us
  matrix products: 33.6 us -> 0 us
  starting transfers between devices: 30.4 us -> 0 us
  between operations: 13.4 us -> 0.01 us
  local copies, waits for them, and re-layouts: 12.2 us -> 2.31 us
  other arithmetic: 6.84 us -> 0 us
    ppermute x8 -> x0, waiting for transfers between devices: 222 us -> none  [shifted(): return lax.ppermute(block, axis, route)]
    reduce_scatter x8 -> x0, waiting for transfers between devices: 121 us -> none  [sum_in_order(): parts = lax.psum_scatter(parts, axes[k], scatter_dimension=0, tiled=True)]
    pallas_call x0 -> x1, Pallas kernels: none -> 76.4 us  [shards(): pl.pallas_call(kernel, out_shape=jax.ShapeDtypeStruct((OCC, SLAB, NAUX),...]
    all_gather x1 -> x0, waiting for transfers between devices: 66.5 us -> none  [shards(): mine = lax.all_gather(integrals, GRP, axis=2, tiled=True)]
    dot_general x12 -> x0, matrix products: 33.6 us -> none  [the longest x4 12.8 us: shards(): jnp.einsum('oap,lbp->olab', own_rows, visiting, preferred_element_type=jn...]
    ppermute x8 -> x0, starting transfers between devices: 30 us -> none  [shifted(): return lax.ppermute(block, axis, route)]
    transpose x4 -> x0, local copies, waits for them, and re-layouts: 9.62 us -> none  [sum_in_order(): parts = parts.transpose(*turns, *range(len(axes), parts.ndim))]
  transfers between devices with their start and end apart: 17 -> 0, of which waited for: 13 -> 0; matrix products, arithmetic and copies ran while one was open for 7% -> 0% of each run, Pallas kernels for 0% -> 0%
where the time goes in v2:
time: 78.9 us; the launch traced here: 78.7 us
  Pallas kernels  76.4 us (97%)
  local copies, waits for them, and re-layouts  2.31 us (3%)
    pallas_call x1, Pallas kernels, shards(): pl.pallas_call(kernel, out_shape=jax.ShapeDtypeStruct((OCC, SLAB, NAUX),...  76.4 us
    unnamed x1, local copies, waits for them, and re-layouts  2.31 us

profile of v2, /device:TPU:1, one launch (start us, length us, event | category | flops | bytes accessed | tf_op | source)
XLA Modules:
  0.0 78.7 jit_solution(14086878221384785021)
XLA Ops:
  0.0 76.4 %amplitudes.1 = f32[4,64,1024]{2,1,0:T(8,128)} custom-call(bf16[4,512,128]{2,1,0:T(8,128)(2,1)} %b_ref.1, f32[128]{0:T(128)} %eo_ref.1, f32[4,128]{1,0:T(4,128)} %bitcast.1, s32[4,4,4]{2,1,0:T(4,128)} %mask_ref.1), custom_call_target="tpu_custom_call" | custom-call | tf_op jit(solution)/shard_map/amplitudes/pallas_call | solution.py:332
  76.4 2.3 %copy.6 = f32[4,64,1024]{2,1,0:T(8,128)} copy(f32[4,64,1024]{2,1,0:T(8,128)} %amplitudes.1) | data formatting | bytes 2097152

commit v3 on v2

--- a/solution.py
+++ b/solution.py
@@ -16,7 +16,7 @@
 SLAB = 64
 SIDE = 512
 KEYS = OCC * QUART
-N_SEM = 72
+N_SEM = 96
 
 
 def kernel(
@@ -97,9 +97,6 @@
 
     cols = slice_of(0)
 
-    def q_part(h):
-        return pl.ds(h * 128, 128)
-
     local = []
     for pr in range(2):
         for t in (1, 3, 2):
@@ -109,30 +106,34 @@
         copy = pltpu.make_async_copy(b_ref.at[pl.ds(2 * pr, 2), rows, :], kb.at[own, pl.ds(2 * pr, 2), :, cols], lsem.at[pr])
         copy.start()
         local.append(copy)
-    for h in range(2):
-        send(("q1", h), b_ref.at[:, part((1 - yl) * HALF + h * 128, 128), :], qb.at[:, q_part(h), cols], lo)
-
-    def queries(h):
-        for t in (1, 3, 2):
-            send(("q2", h, t), b_ref.at[:, part(yl * HALF + h * 128, 128), :], qb.at[:, q_part(h), cols], at_x(t))
-
-    def queries_other(h):
-        ref = qb.at[:, q_part(h), other_slice_of(0)]
-        arrived(("q1", h), ref)
-        for t in (1, 3, 2):
-            send(("q3", h, t), ref, ref, at_x(t))
-
-    def queries_arrived(h):
-        local[2 + h].wait()
-        for t in (1, 3, 2):
-            arrived(("q2", h, t), qb.at[:, q_part(h), slice_of(4 - t)])
-            arrived(("q3", h, t), qb.at[:, q_part(h), other_slice_of(4 - t)])
-
-    queries(0)
-    for h in range(2):
-        copy = pltpu.make_async_copy(b_ref.at[:, part(yl * HALF + h * 128, 128), :], qb.at[:, q_part(h), cols], lsem.at[2 + h])
-        copy.start()
-        local.append(copy)
+    for s in range(4):
+        send(("q1", s), b_ref.at[:, part((1 - yl) * HALF + s * SLAB, SLAB), :], qb.at[:, pl.ds(s * SLAB, SLAB), cols], lo)
+
+    def slab_of(place):
+        return part(place % 4 * SLAB, SLAB)
+
+    def slab(t):
+        return slab_of(x + t)
+
+    def queries(turn):
+        for t in (1, 3, 2):
+            rows = part(yl * HALF + (x + t + turn) % 4 * SLAB, SLAB)
+            send(("q2", turn, t), b_ref.at[:, rows, :], qb.at[:, slab_of(x + t + turn), cols], at_x(t))
+
+    def queries_other(turn):
+        for t in (1, 3, 2):
+            ref = qb.at[:, slab_of(x + t + turn), other_slice_of(0)]
+            send(("q3", turn, t), ref, ref, at_x(t))
+
+    def queries_arrived(turn):
+        for t in (1, 3, 2):
+            arrived(("q2", turn, t), qb.at[:, slab(turn), slice_of(4 - t)])
+            arrived(("q3", turn, t), qb.at[:, slab(turn), other_slice_of(4 - t)])
+
+    queries(2)
+    copy = pltpu.make_async_copy(b_ref.at[:, part(yl * HALF, HALF), :], qb.at[:, :, cols], lsem.at[2])
+    copy.start()
+    local.append(copy)
 
     for s in range(1, 5):
         for o in range(OCC):
@@ -197,18 +198,21 @@
         arrived(("loc", pr), unit(cross, yl, pr))
         to_mate("mcross", cross, pr)
 
-    def hid_ready():
-        ref = unit(diag, 1 - yl, 0)
-        arrived(("hid", 0), ref)
-        send(("lod", 0), ref, ref, lo)
+    def hid_ready(pr):
+        ref = unit(diag, 1 - yl, pr)
+        arrived(("hid", pr), ref)
+        if pr == 0:
+            send(("lod", 0), ref, ref, lo)
+        send(("md1", pr), ref, ref, mate)
 
     def diag_ready(pr):
-        if pr == 0:
-            arrived(("lod", 0), unit(diag, yl, 0))
-        else:
-            arrived(("hid", 1), unit(diag, 1 - yl, 1))
-            arrived(("hie", 1), unit(diag, yl, 1))
-        to_mate("mdiag", diag, pr)
+        ref = unit(diag, yl, pr)
+        arrived(("lod" if pr == 0 else "hie", pr), ref)
+        send(("md2", pr), ref, ref, mate)
+
+    def diag_from_mate(pr):
+        arrived(("md1", pr), unit(mdiag, 1 - yl, pr))
+        arrived(("md2", pr), unit(mdiag, yl, pr))
 
     def from_mate(name, slot, pr):
         arrived((name, pr), whole(slot, pr))
@@ -219,32 +223,33 @@
             value = jnp.where(i == n, values[n], value)
         return value
 
-    def compute(units, a0, na):
+    def compute(tasks):
         def body(i, _):
-            rows = pl.ds(a0, na)
-            q = qb[:, rows, :].reshape(OCC * na, NAUX)
-            nev = nevb[rows, :]
-            nev = jnp.concatenate([nev] * 2, axis=1)
+            wide = len(tasks[0][0])
+            rows = [slab(pick(i, [turns[n] for turns, _ in tasks])) for n in range(wide)]
+            q = jnp.concatenate([qb[:, r, :].reshape(OCC * SLAB, NAUX) for r in rows], axis=0)
+            nevs = [jnp.concatenate([nevb[r, :]] * 2, axis=1) for r in rows]
             total = None
             for n in range(2):
-                slot = pick(i, [unit[n][0] for unit in units])
-                pr = pick(i, [unit[n][1] for unit in units])
+                slot = pick(i, [unit[n][0] for _, unit in tasks])
+                pr = pick(i, [unit[n][1] for _, unit in tasks])
                 d = slot - u
                 keys = kb[slot, pl.ds(2 * pr, 2)].reshape(2 * QUART, NAUX)
                 s = lax.dot_general(q, keys, (((1,), (1,)), ((), ())), preferred_element_type=F32)
                 lanes = part(pr * 256, 256)
                 amps = []
-                for o in range(OCC):
-                    den = rowb[d, pl.ds(o, 1), lanes] - nev
-                    w = wbuf[d, pl.ds(o, 1), lanes]
-                    amps.append((s[o * na : (o + 1) * na] * w / den).astype(BF16))
+                for m in range(wide * OCC):
+                    den = rowb[d, pl.ds(m % OCC, 1), lanes] - nevs[m // OCC]
+                    w = wbuf[d, pl.ds(m % OCC, 1), lanes]
+                    amps.append((s[m * SLAB : (m + 1) * SLAB] * w / den).astype(BF16))
                 amp = jnp.concatenate(amps, axis=0)
                 term = jnp.dot(amp, keys, preferred_element_type=F32)
                 total = term if total is None else total + term
-            acc[:, rows, :] += total.reshape(OCC, na, NAUX)
+            for m in range(wide):
+                acc[:, rows[m], :] += total[m * OCC * SLAB : (m + 1) * OCC * SLAB].reshape(OCC, SLAB, NAUX)
             return 0
 
-        lax.fori_loop(0, len(units), body, 0)
+        lax.fori_loop(0, len(tasks), body, 0)
 
     u0 = ((mown, 0), (mown, 1))
     u1 = ((cross, 0), (below, 0))
@@ -255,11 +260,16 @@
     u6 = ((diag, 0), (diag, 1))
     u7 = ((mdiag, 0), (mdiag, 1))
 
+    near, rest = (2, 1), (3, 0)
+
     own_ready(0)
-    queries_other(0)
+    for s in range(4):
+        arrived(("q1", s), qb.at[:, pl.ds(s * SLAB, SLAB), other_slice_of(0)])
+    queries_other(2)
     own_ready(1)
-    queries(1)
-    queries_other(1)
+    for turn in (1, 3, 0):
+        queries(turn)
+        queries_other(turn)
     lo_ready(0)
     hi_ready(0)
     z_ready(0)
@@ -268,54 +278,49 @@
     z_ready(1)
     for s in range(1, 5):
         arrived(("w", s), wbuf.at[4 + s])
+    local[2].wait()
     from_mate("mown", mown, 0)
     from_mate("mown", mown, 1)
-    queries_arrived(0)
-    compute([u0], 0, 128)
-    zz_ready(0)
-    cross_ready(0)
-    hid_ready()
-    compute([u1], 0, 128)
-    from_mate("mz", mzshare, 0)
-    from_mate("mcross", mcross, 0)
-    compute([u2], 0, 128)
-    zz_ready(1)
-    cross_ready(1)
-    queries_arrived(1)
-    compute([u0, u1, u2], 128, 128)
-    diag_ready(0)
-    from_mate("mz", mzshare, 1)
-    from_mate("mcross", mcross, 1)
-    compute([u3, u4], 0, 256)
-    diag_ready(1)
-    compute([u5], 0, 256)
-    for pr in range(2):
-        from_mate("mdiag", mdiag, pr)
-    late = [u6, u7]
-
-    def slab(t):
-        return part((x + t) % 4 * SLAB, SLAB)
-
-    def finish(t):
-        compute(late, pl.multiple_of((x + t) % 4 * SLAB, SLAB), SLAB)
-
     def push(n, value, dev):
         osend[n] = value.astype(BF16)
         send(("o", n), osend.at[n], orecv.at[n], dev)
 
     first_two, last_two = slice(0, 2), slice(2, 4)
-    finish(2)
+    queries_arrived(2)
+    queries_arrived(1)
+    compute([(near, u0)])
+    zz_ready(0)
+    cross_ready(0)
+    hid_ready(0)
+    compute([(near, u1)])
+    from_mate("mz", mzshare, 0)
+    from_mate("mcross", mcross, 0)
+    compute([(near, u2)])
+    zz_ready(1)
+    cross_ready(1)
+    hid_ready(1)
+    queries_arrived(3)
+    queries_arrived(0)
+    compute([(rest, u0), (rest, u1)])
+    from_mate("mz", mzshare, 1)
+    from_mate("mcross", mcross, 1)
+    compute([(near, u3), (near, u4)])
+    compute([(rest, u2)])
+    diag_ready(0)
+    diag_ready(1)
+    compute([(near, u5), (near, u6)])
+    diag_from_mate(0)
+    diag_from_mate(1)
+    compute([(near, u7)])
     push(0, acc[first_two, slab(2), :], right)
     push(1, acc[last_two, slab(2), :], left)
-    finish(1)
     push(2, acc[last_two, slab(1), :], right)
-    finish(3)
+    compute([(rest, u3), (rest, u4), (rest, u5), (rest, u6), (rest, u7)])
     push(3, acc[first_two, slab(3), :], left)
     arrived(("o", 0), orecv.at[0])
     push(4, acc[first_two, slab(1), :] + orecv[0].astype(F32), right)
     arrived(("o", 1), orecv.at[1])
     push(5, acc[last_two, slab(3), :] + orecv[1].astype(F32), left)
-    finish(0)
     for n in (2, 3):
         arrived(("o", n), orecv.at[n])
     arrived(("o", 4), orecv.at[4])
@@ -331,7 +336,7 @@
     smem = pl.BlockSpec(memory_space=pltpu.SMEM)
     return pl.pallas_call(
         kernel,
-        out_shape=jax.ShapeDtypeStruct((OCC, SLAB, NAUX), F32),
+        out_shape=pltpu.VMEM((OCC, SLAB, NAUX), F32),
         in_specs=[pl.BlockSpec(memory_space=pl.ANY), smem, vmem, smem],
         out_specs=vmem,
         scratch_shapes=[
@@ -346,7 +351,7 @@
             pltpu.VMEM((6, 2, SLAB, NAUX), BF16),
             pltpu.SemaphoreType.DMA((N_SEM,)),
             pltpu.SemaphoreType.DMA((N_SEM,)),
-            pltpu.SemaphoreType.DMA((4,)),
+            pltpu.SemaphoreType.DMA((3,)),
         ],
         compiler_params=pltpu.CompilerParams(
             collective_id=0, has_side_effects=True, vmem_limit_bytes=56 * 1024 * 1024

time: 78.9 us -> 74.4 us (0.943)
  Pallas kernels: 76.4 us -> 73.3 us
  local copies, waits for them, and re-layouts: 2.31 us -> 0.97 us
    pallas_call x1, Pallas kernels: 76.4 us -> 73.3 us  [shards(): pl.pallas_call(kernel, out_shape=pltpu.VMEM((OCC, SLAB, NAUX), F32), in_s...]
    unnamed x1, local copies, waits for them, and re-layouts: 2.31 us -> 0.97 us
where the time goes in v3:
time: 74.4 us; the launch traced here: 74.2 us
  Pallas kernels  73.3 us (99%)
  local copies, waits for them, and re-layouts  0.97 us (1%)
    pallas_call x1, Pallas kernels, shards(): pl.pallas_call(kernel, out_shape=pltpu.VMEM((OCC, SLAB, NAUX), F32), in_s...  73.3 us

profile of v3, /device:TPU:1, one launch (start us, length us, event | category | flops | bytes accessed | tf_op | source)
XLA Modules:
  0.0 74.2 jit_solution(8775742569592766456)
XLA Ops:
  0.0 73.3 %amplitudes.1 = f32[4,64,1024]{2,1,0:T(8,128)S(1)} custom-call(bf16[4,512,128]{2,1,0:T(8,128)(2,1)} %b_ref.1, f32[128]{0:T(128)} %eo_ref.1, f32[4,128]{1,0:T(4,128)} %bitcast.1, s32[4,4,4]{2,1,0:T(4,128)} %mask_ref.1), custom_call_target="tpu_custom_call" | custom-call | tf_op jit(solution)/shard_map/amplitudes/pallas_call | solution.py:337
  73.3 1.0 %copy.6 = f32[4,64,1024]{2,1,0:T(8,128)} copy(f32[4,64,1024]{2,1,0:T(8,128)S(1)} %amplitudes.1) | data formatting | bytes 2097152

commit v4 on v3

--- a/solution.py
+++ b/solution.py
@@ -45,6 +45,7 @@
     lo = (k, 4 * (1 - yl) + x)
     hi = (4 * z + (u + 2) % 4, 4 * (1 - yl) + x)
     right, left = at_x(1), at_x(3)
+    onward = (4 * ((z + nz + 1 - 2 * yh) % nz) + u, g)
 
     barrier = pltpu.get_barrier_semaphore()
     peers = [at_x(1), at_x(2), at_x(3), lo, hi]
@@ -98,14 +99,15 @@
     cols = slice_of(0)
 
     local = []
-    for pr in range(2):
+    chunks = [(0, 1, 0), (1, 1, 0), (2, 2, 1)]
+    for o0, n, _ in chunks:
+        os = pl.ds(o0, n)
         for t in (1, 3, 2):
             rows = part((x + t) % 4 * QUART, QUART)
-            send(("s1", pr, t), b_ref.at[pl.ds(2 * pr, 2), rows, :], kb.at[own, pl.ds(2 * pr, 2), :, cols], at_x(t))
-        rows = part(x * QUART, QUART)
-        copy = pltpu.make_async_copy(b_ref.at[pl.ds(2 * pr, 2), rows, :], kb.at[own, pl.ds(2 * pr, 2), :, cols], lsem.at[pr])
-        copy.start()
-        local.append(copy)
+            send(("s1", o0, t), b_ref.at[os, rows, :], kb.at[own, os, :, cols], at_x(t))
+    copy = pltpu.make_async_copy(b_ref.at[:, part(x * QUART, QUART), :], kb.at[own, :, :, cols], lsem.at[0])
+    copy.start()
+    local.append(copy)
     for s in range(4):
         send(("q1", s), b_ref.at[:, part((1 - yl) * HALF + s * SLAB, SLAB), :], qb.at[:, pl.ds(s * SLAB, SLAB), cols], lo)
 
@@ -131,7 +133,7 @@
             arrived(("q3", turn, t), qb.at[:, slab(turn), other_slice_of(4 - t)])
 
     queries(2)
-    copy = pltpu.make_async_copy(b_ref.at[:, part(yl * HALF, HALF), :], qb.at[:, :, cols], lsem.at[2])
+    copy = pltpu.make_async_copy(b_ref.at[:, part(yl * HALF, HALF), :], qb.at[:, :, cols], lsem.at[1])
     copy.start()
     local.append(copy)
 
@@ -155,34 +157,45 @@
         nevb[pl.ds(h * 128, 128), :] = jnp.transpose(jnp.broadcast_to(row, (128, 128)))
     acc[...] = jnp.zeros_like(acc)
 
+    def rows_unit(slot, half, o0, n):
+        return kb.at[slot, pl.ds(o0, n), :, part(half * SIDE, SIDE)]
+
     def own_ready(pr):
-        local[pr].wait()
-        for t in (1, 3, 2):
-            arrived(("s1", pr, t), kb.at[own, pl.ds(2 * pr, 2), :, slice_of(4 - t)])
-        ref = unit(own, yl, pr)
-        send(("hi", pr), ref, ref, hi)
-        send(("lo", pr), ref, ref, lo)
-        for step in (1, -1):
-            send(("z", step, pr), ref, unit(own - 4 * step, yl, pr), at_z(step))
+        for o0, n, pair in chunks:
+            if pair == pr:
+                if o0 == 0:
+                    local[0].wait()
+                for t in (1, 3, 2):
+                    arrived(("s1", o0, t), kb.at[own, pl.ds(o0, n), :, slice_of(4 - t)])
+                ref = rows_unit(own, yl, o0, n)
+                send(("hi", o0), ref, ref, hi)
+                send(("lo", o0), ref, ref, lo)
+                for step in (1, -1):
+                    send(("z", step, o0), ref, rows_unit(own - 4 * step, yl, o0, n), at_z(step))
+
+    def hop_arrived(name, slot, half, pr):
+        for o0, n, pair in chunks:
+            if pair == pr:
+                arrived(name + (o0,), rows_unit(slot, half, o0, n))
 
     def to_mate(name, slot, pr):
         send((name, pr), whole(slot, pr), whole(slot, pr), mate)
 
     def lo_ready(pr):
         ref = unit(own, 1 - yl, pr)
-        arrived(("lo", pr), ref)
+        hop_arrived(("lo",), own, 1 - yl, pr)
         for step in (1, -1):
             send(("zz", step, pr), ref, unit(own - 4 * step, 1 - yl, pr), at_z(step))
         to_mate("mown", own, pr)
 
     def hi_ready(pr):
         ref = unit(cross, 1 - yl, pr)
-        arrived(("hi", pr), ref)
+        hop_arrived(("hi",), cross, 1 - yl, pr)
         send(("loc", pr), ref, ref, lo)
 
     def z_ready(pr):
         for step in (1, -1):
-            arrived(("z", step, pr), unit(own - 4 * step, yl, pr))
+            hop_arrived(("z", step), own - 4 * step, yl, pr)
         ref = unit(dsend, yl, pr)
         send(("hid", pr), ref, ref, hi)
 
@@ -196,18 +209,26 @@
 
     def cross_ready(pr):
         arrived(("loc", pr), unit(cross, yl, pr))
+        if pr == 0:
+            ref = rows_unit(cross, yl, 1, 1)
+            send(("zd",), ref, rows_unit(cross - s4, yl, 1, 1), onward)
         to_mate("mcross", cross, pr)
 
     def hid_ready(pr):
         ref = unit(diag, 1 - yl, pr)
         arrived(("hid", pr), ref)
         if pr == 0:
-            send(("lod", 0), ref, ref, lo)
+            first = rows_unit(diag, 1 - yl, 0, 1)
+            send(("lod", 0), first, first, lo)
         send(("md1", pr), ref, ref, mate)
 
     def diag_ready(pr):
         ref = unit(diag, yl, pr)
-        arrived(("lod" if pr == 0 else "hie", pr), ref)
+        if pr == 0:
+            arrived(("lod", 0), rows_unit(diag, yl, 0, 1))
+            arrived(("zd",), rows_unit(diag, yl, 1, 1))
+        else:
+            arrived(("hie", 1), ref)
         send(("md2", pr), ref, ref, mate)
 
     def diag_from_mate(pr):
@@ -278,7 +299,7 @@
     z_ready(1)
     for s in range(1, 5):
         arrived(("w", s), wbuf.at[4 + s])
-    local[2].wait()
+    local[1].wait()
     from_mate("mown", mown, 0)
     from_mate("mown", mown, 1)
     def push(n, value, dev):
@@ -301,26 +322,27 @@
     hid_ready(1)
     queries_arrived(3)
     queries_arrived(0)
-    compute([(rest, u0), (rest, u1)])
+    compute([(rest, u0)])
     from_mate("mz", mzshare, 1)
     from_mate("mcross", mcross, 1)
     compute([(near, u3), (near, u4)])
-    compute([(rest, u2)])
     diag_ready(0)
     diag_ready(1)
     compute([(near, u5), (near, u6)])
     diag_from_mate(0)
     diag_from_mate(1)
-    compute([(near, u7)])
+    compute([((2,), u7)])
     push(0, acc[first_two, slab(2), :], right)
     push(1, acc[last_two, slab(2), :], left)
+    compute([((1,), u7)])
     push(2, acc[last_two, slab(1), :], right)
-    compute([(rest, u3), (rest, u4), (rest, u5), (rest, u6), (rest, u7)])
+    compute([((3,), u1), ((3,), u2), ((3,), u3), ((3,), u4), ((3,), u5), ((3,), u6), ((3,), u7)])
     push(3, acc[first_two, slab(3), :], left)
     arrived(("o", 0), orecv.at[0])
     push(4, acc[first_two, slab(1), :] + orecv[0].astype(F32), right)
     arrived(("o", 1), orecv.at[1])
     push(5, acc[last_two, slab(3), :] + orecv[1].astype(F32), left)
+    compute([((0,), u1), ((0,), u2), ((0,), u3), ((0,), u4), ((0,), u5), ((0,), u6), ((0,), u7)])
     for n in (2, 3):
         arrived(("o", n), orecv.at[n])
     arrived(("o", 4), orecv.at[4])
@@ -351,7 +373,7 @@
             pltpu.VMEM((6, 2, SLAB, NAUX), BF16),
             pltpu.SemaphoreType.DMA((N_SEM,)),
             pltpu.SemaphoreType.DMA((N_SEM,)),
-            pltpu.SemaphoreType.DMA((3,)),
+            pltpu.SemaphoreType.DMA((2,)),
         ],
         compiler_params=pltpu.CompilerParams(
             collective_id=0, has_side_effects=True, vmem_limit_bytes=56 * 1024 * 1024

time: 74.4 us -> 72.8 us (0.978)
  Pallas kernels: 73.3 us -> 71.7 us
    pallas_call x1, Pallas kernels: 73.3 us -> 71.7 us  [shards(): pl.pallas_call(kernel, out_shape=pltpu.VMEM((OCC, SLAB, NAUX), F32), in_s...]
where the time goes in v4:
time: 72.8 us; the launch traced here: 72.7 us
  Pallas kernels  71.7 us (98%)
  local copies, waits for them, and re-layouts  0.97 us (1%)
    pallas_call x1, Pallas kernels, shards(): pl.pallas_call(kernel, out_shape=pltpu.VMEM((OCC, SLAB, NAUX), F32), in_s...  71.7 us

profile of v4, /device:TPU:1, one launch (start us, length us, event | category | flops | bytes accessed | tf_op | source)
XLA Modules:
  0.0 72.7 jit_solution(16223045742508571854)
XLA Ops:
  0.0 71.7 %amplitudes.1 = f32[4,64,1024]{2,1,0:T(8,128)S(1)} custom-call(bf16[4,512,128]{2,1,0:T(8,128)(2,1)} %b_ref.1, f32[128]{0:T(128)} %eo_ref.1, f32[4,128]{1,0:T(4,128)} %bitcast.1, s32[4,4,4]{2,1,0:T(4,128)} %mask_ref.1), custom_call_target="tpu_custom_call" | custom-call | tf_op jit(solution)/shard_map/amplitudes/pallas_call | solution.py:359
  71.7 1.0 %copy.6 = f32[4,64,1024]{2,1,0:T(8,128)} copy(f32[4,64,1024]{2,1,0:T(8,128)S(1)} %amplitudes.1) | data formatting | bytes 2097152

commit v5 on v4

--- a/solution.py
+++ b/solution.py
@@ -281,8 +281,6 @@
     u6 = ((diag, 0), (diag, 1))
     u7 = ((mdiag, 0), (mdiag, 1))
 
-    near, rest = (2, 1), (3, 0)
-
     own_ready(0)
     for s in range(4):
         arrived(("q1", s), qb.at[:, pl.ds(s * SLAB, SLAB), other_slice_of(0)])
@@ -309,40 +307,43 @@
     first_two, last_two = slice(0, 2), slice(2, 4)
     queries_arrived(2)
     queries_arrived(1)
-    compute([(near, u0)])
+    compute([((2, 1), u0)])
     zz_ready(0)
     cross_ready(0)
     hid_ready(0)
-    compute([(near, u1)])
+    compute([((2, 1), u1)])
     from_mate("mz", mzshare, 0)
     from_mate("mcross", mcross, 0)
-    compute([(near, u2)])
+    compute([((2, 1), u2)])
     zz_ready(1)
     cross_ready(1)
     hid_ready(1)
     queries_arrived(3)
-    queries_arrived(0)
-    compute([(rest, u0)])
+    compute([((3,), u0), ((3,), u1)])
     from_mate("mz", mzshare, 1)
     from_mate("mcross", mcross, 1)
-    compute([(near, u3), (near, u4)])
+    compute([((2, 1), u3)])
+    compute([((2,), u4)])
+    compute([((3,), u2)])
     diag_ready(0)
     diag_ready(1)
-    compute([(near, u5), (near, u6)])
+    compute([((2,), u5), ((2,), u6)])
     diag_from_mate(0)
     diag_from_mate(1)
     compute([((2,), u7)])
     push(0, acc[first_two, slab(2), :], right)
     push(1, acc[last_two, slab(2), :], left)
-    compute([((1,), u7)])
+    compute([((1, 3), u5), ((1, 3), u6), ((1, 3), u7)])
+    compute([((1,), u4)])
     push(2, acc[last_two, slab(1), :], right)
-    compute([((3,), u1), ((3,), u2), ((3,), u3), ((3,), u4), ((3,), u5), ((3,), u6), ((3,), u7)])
+    compute([((3,), u3), ((3,), u4)])
     push(3, acc[first_two, slab(3), :], left)
     arrived(("o", 0), orecv.at[0])
     push(4, acc[first_two, slab(1), :] + orecv[0].astype(F32), right)
     arrived(("o", 1), orecv.at[1])
     push(5, acc[last_two, slab(3), :] + orecv[1].astype(F32), left)
-    compute([((0,), u1), ((0,), u2), ((0,), u3), ((0,), u4), ((0,), u5), ((0,), u6), ((0,), u7)])
+    queries_arrived(0)
+    compute([((0,), u0), ((0,), u1), ((0,), u2), ((0,), u3), ((0,), u4), ((0,), u5), ((0,), u6), ((0,), u7)])
     for n in (2, 3):
         arrived(("o", n), orecv.at[n])
     arrived(("o", 4), orecv.at[4])

time: 72.8 us -> 71.9 us (0.988)
  Pallas kernels: 71.7 us -> 70.8 us
    pallas_call x1, Pallas kernels: 71.7 us -> 70.8 us  [shards(): pl.pallas_call(kernel, out_shape=pltpu.VMEM((OCC, SLAB, NAUX), F32), in_s...]
where the time goes in v5:
time: 71.9 us; the launch traced here: 71.7 us
  Pallas kernels  70.8 us (98%)
  local copies, waits for them, and re-layouts  0.97 us (1%)
    pallas_call x1, Pallas kernels, shards(): pl.pallas_call(kernel, out_shape=pltpu.VMEM((OCC, SLAB, NAUX), F32), in_s...  70.8 us

profile of v5, /device:TPU:1, one launch (start us, length us, event | category | flops | bytes accessed | tf_op | source)
XLA Modules:
  0.0 71.7 jit_solution(15265257565806393515)
XLA Ops:
  0.0 70.8 %amplitudes.1 = f32[4,64,1024]{2,1,0:T(8,128)S(1)} custom-call(bf16[4,512,128]{2,1,0:T(8,128)(2,1)} %b_ref.1, f32[128]{0:T(128)} %eo_ref.1, f32[4,128]{1,0:T(4,128)} %bitcast.1, s32[4,4,4]{2,1,0:T(4,128)} %mask_ref.1), custom_call_target="tpu_custom_call" | custom-call | tf_op jit(solution)/shard_map/amplitudes/pallas_call | solution.py:360
  70.8 1.0 %copy.6 = f32[4,64,1024]{2,1,0:T(8,128)} copy(f32[4,64,1024]{2,1,0:T(8,128)S(1)} %amplitudes.1) | data formatting | bytes 2097152

commit v6 on v5

--- a/solution.py
+++ b/solution.py
@@ -339,17 +339,23 @@
     compute([((3,), u3), ((3,), u4)])
     push(3, acc[first_two, slab(3), :], left)
     arrived(("o", 0), orecv.at[0])
-    push(4, acc[first_two, slab(1), :] + orecv[0].astype(F32), right)
+    for r in range(2):
+        osend[4, r] = (acc[r, slab(1), :] + orecv[0, r].astype(F32)).astype(BF16)
+        send(("b", 4, r), osend.at[4, r], orecv.at[4, r], right)
     arrived(("o", 1), orecv.at[1])
-    push(5, acc[last_two, slab(3), :] + orecv[1].astype(F32), left)
+    for r in range(2):
+        osend[5, r] = (acc[2 + r, slab(3), :] + orecv[1, r].astype(F32)).astype(BF16)
+        send(("b", 5, r), osend.at[5, r], orecv.at[5, r], left)
     queries_arrived(0)
     compute([((0,), u0), ((0,), u1), ((0,), u2), ((0,), u3), ((0,), u4), ((0,), u5), ((0,), u6), ((0,), u7)])
     for n in (2, 3):
         arrived(("o", n), orecv.at[n])
-    arrived(("o", 4), orecv.at[4])
-    out_ref[first_two] = acc[first_two, slab(0), :] + orecv[3].astype(F32) + orecv[4].astype(F32)
-    arrived(("o", 5), orecv.at[5])
-    out_ref[last_two] = acc[last_two, slab(0), :] + orecv[2].astype(F32) + orecv[5].astype(F32)
+    out_ref[first_two] = acc[first_two, slab(0), :] + orecv[3].astype(F32)
+    out_ref[last_two] = acc[last_two, slab(0), :] + orecv[2].astype(F32)
+    for r in range(2):
+        for n, o in ((4, r), (5, 2 + r)):
+            arrived(("b", n, r), orecv.at[n, r])
+            out_ref[o] = out_ref[o] + orecv[n, r].astype(F32)
     for copy in sent:
         copy.wait_send()
 

time: 71.9 us -> 71.8 us (level)
  no operation moved by 1% of the time
where the time goes in v6:
time: 71.8 us; the launch traced here: 71.7 us
  Pallas kernels  70.7 us (98%)
  local copies, waits for them, and re-layouts  0.97 us (1%)
    pallas_call x1, Pallas kernels, shards(): pl.pallas_call(kernel, out_shape=pltpu.VMEM((OCC, SLAB, NAUX), F32), in_s...  70.7 us

profile of v6, /device:TPU:1, one launch (start us, length us, event | category | flops | bytes accessed | tf_op | source)
XLA Modules:
  0.0 71.7 jit_solution(12736111374026076943)
XLA Ops:
  0.0 70.7 %amplitudes.1 = f32[4,64,1024]{2,1,0:T(8,128)S(1)} custom-call(bf16[4,512,128]{2,1,0:T(8,128)(2,1)} %b_ref.1, f32[128]{0:T(128)} %eo_ref.1, f32[4,128]{1,0:T(4,128)} %bitcast.1, s32[4,4,4]{2,1,0:T(4,128)} %mask_ref.1), custom_call_target="tpu_custom_call" | custom-call | tf_op jit(solution)/shard_map/amplitudes/pallas_call | solution.py:366
  70.7 1.0 %copy.6 = f32[4,64,1024]{2,1,0:T(8,128)} copy(f32[4,64,1024]{2,1,0:T(8,128)S(1)} %amplitudes.1) | data formatting | bytes 2097152
